TPU v7x, 32 devices: a whole 2x2x4 slice. The times are simulated.
32 devices in a mesh: dp: 8 (over y, x, core), tensor: 4 (over z).
Axes of the slice: x: 2, y: 2, z: 4, core: 2. Of those that a mesh axis runs over, the one named last changes fastest.
Arguments:
- tokens: bfloat16 [8192, 2048], P(('dp', 'tensor')), may hold values from -6 to 6
- segments: int32 [8192], P('dp'), may hold values from 0 to 1023, as said below
- positions: int32 [8192], P('dp'), may hold values from 0 to 1023, as said below
- norm_attn: float32 [2048], replicated, may hold values from 0.25 to 1.75
- w_query: bfloat16 [2048, 2048], P('dp', 'tensor'), may hold values from -0.125 to 0.125
- w_key: bfloat16 [2048, 512], P('dp', 'tensor'), may hold values from -0.125 to 0.125
- w_value: bfloat16 [2048, 512], P('dp', 'tensor'), may hold values from -0.125 to 0.125
- w_out: bfloat16 [2048, 2048], P('tensor', 'dp'), may hold values from -0.375 to 0.375
- norm_mlp: float32 [2048], replicated, may hold values from 0.25 to 1.75
- w_gate: bfloat16 [2048, 8192], P('dp', 'tensor'), may hold values from -0.125 to 0.125
- w_up: bfloat16 [2048, 8192], P('dp', 'tensor'), may hold values from -0.125 to 0.125
- w_down: bfloat16 [8192, 2048], P('tensor', 'dp'), may hold values from -0.09375 to 0.09375
- cotangent: bfloat16 [8192, 2048], P(('dp', 'tensor')), may hold values from -6 to 6
Outputs:
- layer_out: bfloat16 [8192, 2048], P(('dp', 'tensor'))
- input_grad: float32 [8192, 2048], P(('dp', 'tensor'))
- grad_norm_attn: float32 [2048], replicated
- grad_query: float32 [2048, 2048], P('dp', 'tensor')
- grad_key: float32 [2048, 512], P('dp', 'tensor')
- grad_value: float32 [2048, 512], P('dp', 'tensor')
- grad_output: float32 [2048, 2048], P('tensor', 'dp')
- grad_norm_mlp: float32 [2048], replicated
- grad_gate: float32 [2048, 8192], P('dp', 'tensor')
- grad_up: float32 [2048, 8192], P('dp', 'tensor')
- grad_down: float32 [8192, 2048], P('tensor', 'dp')
Inputs may be any that keep to these rules, and one draw needn't show every extreme that they name: `segments`: within each sequence of 1024 tokens, a token's label is the place in that sequence of its document's first token, so labels never fall along a sequence; the first sequence of all is a single document, and the last token of the last sequence starts a document of its own. `positions`: each token's position counts from 0 at its document's first token.
All inputs are finite; a program needn't handle non-finite values.
Results may differ from a plain program's by a relative error of at most 0.022.
Values may be sent and summed in bfloat16 or wider, within the bound.
No kernel may reach another device: no remote copies, remote signals or barrier semaphores. Data moves between devices by JAX's collectives and lax.ppermute only.
A program may use at most 192 MiB of HBM per device.

v0:
```python
from functools import partial
import math
import jax
import jax.numpy as jnp
from jax import lax
from jax.sharding import PartitionSpec as P

QH = 32
KVH = 8
HD = 64
LEN = 1024


def rms_scale(values, norm_gain):
    inverse = lax.rsqrt(jnp.mean(values * values, axis=-1, keepdims=True) + 1e-05)
    return values * inverse * norm_gain


def rotary_tables(positions):
    freq_index = jnp.arange(HD // 2, dtype=jnp.int32).astype(jnp.float32)
    inverse = jnp.exp(freq_index * (-2.0 * math.log(500000.0) / HD))
    angles = positions.astype(jnp.float32)[:, None] * inverse[None, :]
    return (jnp.cos(angles), jnp.sin(angles))


def rotate(values, cosine_table, sine_table):
    half_width = values.shape[-1] // 2
    lower_half = values[..., :half_width]
    upper_half = values[..., half_width:]
    cosine_rows = cosine_table[:, None, :]
    sine_rows = sine_table[:, None, :]
    return jnp.concatenate(
        [
            lower_half * cosine_rows - upper_half * sine_rows,
            upper_half * cosine_rows + lower_half * sine_rows,
        ],
        axis=-1,
    )


def silu_product(gate_values, up_values):
    return jax.nn.silu(gate_values) * up_values


def local(
    tokens,
    segments,
    positions,
    norm_attn,
    w_query,
    w_key,
    w_value,
    w_out,
    norm_mlp,
    w_gate,
    w_up,
    w_down,
    cotangent,
):
    kv_local = w_key.shape[1] // HD
    per_group = QH // KVH
    block_rows = min(512, LEN)
    score_scale = 1.0 / math.sqrt(HD)
    inputs = tokens.astype(jnp.float32)
    normed_local = rms_scale(inputs, norm_attn).astype(jnp.bfloat16)
    normed_in = lax.all_gather(normed_local, "tensor", axis=0, tiled=True)
    query_all, key_all, value_all, out_all = (
        lax.all_gather(w_query, "dp", axis=0, tiled=True),
        lax.all_gather(w_key, "dp", axis=0, tiled=True),
        lax.all_gather(w_value, "dp", axis=0, tiled=True),
        lax.all_gather(w_out, "dp", axis=1, tiled=True),
    )
    group_rows = normed_in.shape[0]
    block_count = group_rows // block_rows
    cosine_table, sine_table = rotary_tables(positions)
    rotate_here = partial(rotate, cosine_table=cosine_table, sine_table=sine_table)
    query_raw = jnp.dot(normed_in, query_all, preferred_element_type=jnp.float32).reshape(
        group_rows, kv_local * per_group, HD
    )
    key_raw = jnp.dot(normed_in, key_all, preferred_element_type=jnp.float32).reshape(
        group_rows, kv_local, HD
    )
    all_queries = (
        rotate_here(query_raw).astype(jnp.bfloat16).reshape(group_rows, kv_local, per_group, HD)
    )
    all_keys = rotate_here(key_raw).astype(jnp.bfloat16)
    all_values = (
        jnp.dot(normed_in, value_all, preferred_element_type=jnp.float32)
        .astype(jnp.bfloat16)
        .reshape(group_rows, kv_local, HD)
    )
    place_index = jnp.arange(LEN, dtype=jnp.int32)

    def block_scores(block_index):
        row_start = block_index * block_rows
        seq_start = row_start // LEN * LEN
        query_rows = lax.dynamic_slice_in_dim(all_queries, row_start, block_rows, 0)
        query_segs = lax.dynamic_slice_in_dim(segments, row_start, block_rows, 0)
        query_place = row_start - seq_start + jnp.arange(block_rows, dtype=jnp.int32)
        allowed = (place_index[None, :] <= query_place[:, None]) & (
            segments[None, :] == query_segs[:, None]
        )
        scores = (
            jnp.einsum("qhgd,khd->hgqk", query_rows, all_keys, preferred_element_type=jnp.float32)
            * score_scale
        )
        return (jnp.where(allowed, scores, -1e30), query_rows, all_keys, all_values, seq_start)

    def forward_block(block_index):
        scores, query_rows, near_keys, near_values, seq_start = block_scores(block_index)
        row_peak = jnp.max(scores, axis=-1, keepdims=True)
        row_total = jnp.sum(jnp.exp(scores - row_peak), axis=-1, keepdims=True)
        log_total = row_peak + jnp.log(row_total)
        attn_probs = jnp.exp(scores - log_total).astype(jnp.bfloat16)
        context_block = jnp.einsum(
            "hgqk,khd->qhgd", attn_probs, near_values, preferred_element_type=jnp.float32
        )
        return (context_block.reshape(block_rows, -1).astype(jnp.bfloat16), log_total)

    context, log_totals = lax.map(forward_block, jnp.arange(block_count, dtype=jnp.int32))
    context = context.reshape(group_rows, -1)
    attn_branch = lax.psum_scatter(
        jnp.dot(context, out_all, preferred_element_type=jnp.float32).astype(jnp.bfloat16),
        "tensor",
        scatter_dimension=0,
        tiled=True,
    ).astype(jnp.float32)
    middle = inputs + attn_branch
    normed_mid_local = rms_scale(middle, norm_mlp).astype(jnp.bfloat16)
    normed_mid = lax.all_gather(normed_mid_local, "tensor", axis=0, tiled=True)
    gate_all, up_all, down_all = (
        lax.all_gather(w_gate, "dp", axis=0, tiled=True),
        lax.all_gather(w_up, "dp", axis=0, tiled=True),
        lax.all_gather(w_down, "dp", axis=1, tiled=True),
    )
    gate_values = jnp.dot(normed_mid, gate_all, preferred_element_type=jnp.float32)
    up_values = jnp.dot(normed_mid, up_all, preferred_element_type=jnp.float32)
    hidden = silu_product(gate_values, up_values).astype(jnp.bfloat16)
    mlp_branch = lax.psum_scatter(
        jnp.dot(hidden, down_all, preferred_element_type=jnp.float32).astype(jnp.bfloat16),
        "tensor",
        scatter_dimension=0,
        tiled=True,
    ).astype(jnp.float32)
    layer_out = (middle + mlp_branch).astype(jnp.bfloat16)
    cot_all = lax.all_gather(cotangent, "tensor", axis=0, tiled=True)
    d_hidden = jnp.einsum("rd,fd->rf", cot_all, down_all, preferred_element_type=jnp.float32)
    silu_back = jax.vjp(silu_product, gate_values, up_values)[1]
    d_gate32, d_up32 = silu_back(d_hidden)
    d_gate = d_gate32.astype(jnp.bfloat16)
    d_up = d_up32.astype(jnp.bfloat16)
    gate_part = jnp.einsum("rd,rf->df", normed_mid, d_gate, preferred_element_type=jnp.float32)
    up_part = jnp.einsum("rd,rf->df", normed_mid, d_up, preferred_element_type=jnp.float32)
    down_part = jnp.einsum("rf,rd->fd", hidden, cot_all, preferred_element_type=jnp.float32)
    d_normed_mid = lax.psum_scatter(
        (
            jnp.einsum("rf,df->rd", d_gate, gate_all, preferred_element_type=jnp.float32)
            + jnp.einsum("rf,df->rd", d_up, up_all, preferred_element_type=jnp.float32)
        ).astype(jnp.bfloat16),
        "tensor",
        scatter_dimension=0,
        tiled=True,
    ).astype(jnp.float32)
    mid_back = jax.vjp(rms_scale, middle, norm_mlp)[1]
    d_middle_norm, mlp_gain_part = mid_back(d_normed_mid)
    d_middle = cotangent.astype(jnp.float32) + d_middle_norm
    d_branch = lax.all_gather(d_middle.astype(jnp.bfloat16), "tensor", axis=0, tiled=True)
    out_part = jnp.einsum("rc,rd->cd", context, d_branch, preferred_element_type=jnp.float32)
    d_context = jnp.einsum(
        "rd,cd->rc", d_branch, out_all, preferred_element_type=jnp.float32
    ).astype(jnp.bfloat16)
    d_context = d_context.reshape(group_rows, kv_local, per_group, HD)

    def backward_block(grad_carry, block_index):
        key_grads, value_grads = grad_carry
        scores, query_rows, near_keys, near_values, seq_start = block_scores(block_index)
        probs_full = jnp.exp(scores - log_totals[block_index])
        attn_probs = probs_full.astype(jnp.bfloat16)
        d_rows = lax.dynamic_slice_in_dim(d_context, block_index * block_rows, block_rows, 0)
        d_probs = jnp.einsum(
            "qhgd,khd->hgqk", d_rows, near_values, preferred_element_type=jnp.float32
        )
        d_scores = (
            probs_full * (d_probs - jnp.sum(probs_full * d_probs, axis=-1, keepdims=True))
        ).astype(jnp.bfloat16)
        d_queries = (
            jnp.einsum("hgqk,khd->qhgd", d_scores, near_keys, preferred_element_type=jnp.float32)
            * score_scale
        )
        d_keys = (
            jnp.einsum("hgqk,qhgd->khd", d_scores, query_rows, preferred_element_type=jnp.float32)
            * score_scale
        )
        d_values = jnp.einsum(
            "hgqk,qhgd->khd", attn_probs, d_rows, preferred_element_type=jnp.float32
        )
        old_keys = key_grads
        key_grads = old_keys + d_keys
        old_values = value_grads
        value_grads = old_values + d_values
        return ((key_grads, value_grads), d_queries)

    empty_grads = jnp.zeros((group_rows, kv_local, HD), jnp.float32)
    kv_grads, query_grads = lax.scan(
        backward_block, (empty_grads, empty_grads), jnp.arange(block_count, dtype=jnp.int32)
    )
    query_grads = query_grads.reshape(group_rows, kv_local * per_group, HD)
    query_back = jax.vjp(rotate_here, query_raw)[1]
    key_back = jax.vjp(rotate_here, key_raw)[1]
    d_query_raw = query_back(query_grads)[0].astype(jnp.bfloat16).reshape(group_rows, -1)
    d_key_raw = key_back(kv_grads[0])[0].astype(jnp.bfloat16).reshape(group_rows, -1)
    d_value_raw = kv_grads[1].astype(jnp.bfloat16).reshape(group_rows, -1)
    query_part = jnp.einsum("rd,rc->dc", normed_in, d_query_raw, preferred_element_type=jnp.float32)
    key_part = jnp.einsum("rd,rc->dc", normed_in, d_key_raw, preferred_element_type=jnp.float32)
    value_part = jnp.einsum("rd,rc->dc", normed_in, d_value_raw, preferred_element_type=jnp.float32)
    query_rows = d_query_raw
    d_normed_in = lax.psum_scatter(
        (
            jnp.einsum("rc,dc->rd", query_rows, query_all, preferred_element_type=jnp.float32)
            + jnp.einsum("rc,dc->rd", d_key_raw, key_all, preferred_element_type=jnp.float32)
            + jnp.einsum("rc,dc->rd", d_value_raw, value_all, preferred_element_type=jnp.float32)
        ).astype(jnp.bfloat16),
        "tensor",
        scatter_dimension=0,
        tiled=True,
    ).astype(jnp.float32)
    in_back = jax.vjp(rms_scale, inputs, norm_attn)[1]
    d_input_norm, attn_gain_part = in_back(d_normed_in)
    input_grad = d_middle + d_input_norm
    grad_norm_attn, grad_norm_mlp = lax.psum((attn_gain_part, mlp_gain_part), ("dp", "tensor"))
    grad_query, grad_key, grad_value, grad_output, grad_gate, grad_up, grad_down = (
        lax.psum_scatter(
            query_part.astype(jnp.bfloat16), "dp", scatter_dimension=0, tiled=True
        ).astype(jnp.float32),
        lax.psum_scatter(
            key_part.astype(jnp.bfloat16), "dp", scatter_dimension=0, tiled=True
        ).astype(jnp.float32),
        lax.psum_scatter(
            value_part.astype(jnp.bfloat16), "dp", scatter_dimension=0, tiled=True
        ).astype(jnp.float32),
        lax.psum_scatter(
            out_part.astype(jnp.bfloat16), "dp", scatter_dimension=1, tiled=True
        ).astype(jnp.float32),
        lax.psum_scatter(
            gate_part.astype(jnp.bfloat16), "dp", scatter_dimension=0, tiled=True
        ).astype(jnp.float32),
        lax.psum_scatter(
            up_part.astype(jnp.bfloat16), "dp", scatter_dimension=0, tiled=True
        ).astype(jnp.float32),
        lax.psum_scatter(
            down_part.astype(jnp.bfloat16), "dp", scatter_dimension=1, tiled=True
        ).astype(jnp.float32),
    )
    return (
        layer_out,
        input_grad,
        grad_norm_attn,
        grad_query,
        grad_key,
        grad_value,
        grad_output,
        grad_norm_mlp,
        grad_gate,
        grad_up,
        grad_down,
    )


def solution(mesh):
    in_specs = (
        P(("dp", "tensor"), None),
        P("dp"),
        P("dp"),
        P(),
        P("dp", "tensor"),
        P("dp", "tensor"),
        P("dp", "tensor"),
        P("tensor", "dp"),
        P(),
        P("dp", "tensor"),
        P("dp", "tensor"),
        P("tensor", "dp"),
        P(("dp", "tensor"), None),
    )
    out_specs = (
        P(("dp", "tensor"), None),
        P(("dp", "tensor"), None),
        P(),
        P("dp", "tensor"),
        P("dp", "tensor"),
        P("dp", "tensor"),
        P("tensor", "dp"),
        P(),
        P("dp", "tensor"),
        P("dp", "tensor"),
        P("tensor", "dp"),
    )
    return jax.shard_map(local, mesh=mesh, in_specs=in_specs, out_specs=out_specs, check_vma=False)
```

profile of v0, /device:TPU:0, one launch (start us, length us, event | category | flops | bytes accessed | tf_op | source)
XLA Modules:
  0.0 1351.4 jit_solution(8502099795112230766)
XLA Ops:
  14.0 11.3 all_gather.35
  25.4 9.8 all_gather.36
  35.7 60.3 %all-gather.10.cloned.1.call-done = bf16[1024,2048]{1,0:T(8,128)(2,1)} async-done(((bf16[256,2048]{1,0:T(8,128)(2,1)}), bf16[1024,2048]{1,0:T(8,128)(2,1)}) %all-gather.10.cloned.1.call-update) | async-done | bytes 4194320 | tf_op jit(solution)/shard_map/all_gather | solution.py:66
  96.0 3.7 fusion.76
  99.8 24.4 %all-gather.12.cloned.1.call-done = bf16[2048,512]{1,0:T(8,128)(2,1)} async-done(((bf16[256,512]{1,0:T(8,128)(2,1)}), bf16[2048,512]{1,0:T(8,128)(2,1)}) %all-gather.12.cloned.1.call-update) | async-done | bytes 2097168 | tf_op jit(solution)/shard_map/all_gather | solution.py:68
  124.2 5.2 fusion.75
  133.2 30.5 %while.32 = (s32[]{:T(128)}, bf16[2,512,512]{2,1,0:T(8,128)(2,1)}, f32[2,2,4,512,1]{3,2,1,4,0:T(4,128)}, s32[2]{0:T(128)S(1)}, s32[1024]{0:T(1024)S(1)}, /*index...) while((s32[]{:T(128)}, bf16[2,512,512]{2,1,0:T(8,128)(2,1)}, ...), condition=%wide.region_4.5_spmd.clone, body=%wide.region_1.4_spmd.clone.sunk | while | flops 1121710592 | bytes 56244616 | solution.py:120
  135.4 2.8 bitcast_reduce_fusion.2
  138.2 4.3 fusion.149
  143.2 4.4 fusion.150
  150.5 2.8 bitcast_reduce_fusion.2
  153.3 4.3 fusion.149
  158.3 4.4 fusion.150
  163.7 6.9 convolution_convert_fusion.4
  171.3 76.3 %reduce-scatter.12.cloned.1.call-done = bf16[256,2048]{1,0:T(8,128)(2,1)} async-done(((bf16[1024,2048]{1,0:T(8,128)(2,1)}), bf16[256,2048]{1,0:T(8,128)(2,1)}) %reduce-scatter.12.cloned.1.call-update) | async-done | bytes 1048592 | tf_op jit(solution)/shard_map/reduce_scatter | solution.py:122
  254.2 50.0 %all-gather.20.cloned.1.call-done = bf16[2048,2048]{1,0:T(8,128)(2,1)} async-done(((bf16[256,2048]{1,0:T(8,128)(2,1)}), bf16[2048,2048]{1,0:T(8,128)(2,1)}) %all-gather.20.cloned.1.call-update) | async-done | bytes 8388624 | tf_op jit(solution)/shard_map/all_gather | solution.py:133
  304.1 82.8 %all-gather.16.cloned.1.call-done = bf16[1024,2048]{1,0:T(8,128)(2,1)} async-done(((bf16[256,2048]{1,0:T(8,128)(2,1)}), bf16[1024,2048]{1,0:T(8,128)(2,1)}) %all-gather.16.cloned.1.call-update) | async-done | bytes 4194320 | tf_op jit(solution)/shard_map/all_gather | solution.py:130
  386.9 14.9 %fusion.78 = f32[1024,2048]{1,0:T(8,128)} fusion(bf16[1024,2048]{1,0:T(8,128)(2,1)} %all-gather.16.cloned.1.call-done, bf16[2048,2048]{1,0:T(8,128)(2,1)} %all-gather.20.cloned.1.call-done), kind=kOutput, calls=%fused_computation.135 | convolution fusion | flops 8589934592 | bytes 20971520 | tf_op jit(solution)/shard_map/dot_general | solution.py:137
  401.8 39.8 %all-gather.18.cloned.1.call-done = bf16[2048,2048]{1,0:T(8,128)(2,1)} async-done(((bf16[256,2048]{1,0:T(8,128)(2,1)}), bf16[2048,2048]{1,0:T(8,128)(2,1)}) %all-gather.18.cloned.1.call-update) | async-done | bytes 8388624 | tf_op jit(solution)/shard_map/all_gather | solution.py:132
  441.6 14.4 %fusion.77 = f32[1024,2048]{1,0:T(8,128)} fusion(bf16[1024,2048]{1,0:T(8,128)(2,1)} %all-gather.16.cloned.1.call-done, bf16[2048,2048]{1,0:T(8,128)(2,1)} %all-gather.18.cloned.1.call-done), kind=kOutput, calls=%fused_computation.134 | convolution fusion | flops 8589934592 | bytes 20971520 | tf_op jit(solution)/shard_map/dot_general | solution.py:136
  455.9 67.9 %all-gather.24.cloned.1.call-done = bf16[1024,2048]{1,0:T(8,128)(2,1)} async-done(((bf16[256,2048]{1,0:T(8,128)(2,1)}), bf16[1024,2048]{1,0:T(8,128)(2,1)}) %all-gather.24.cloned.1.call-update) | async-done | bytes 4194320 | tf_op jit(solution)/shard_map/all_gather | solution.py:146
  523.9 56.3 %all-gather.22.cloned.1.call-done = bf16[2048,2048]{1,0:T(8,128)(2,1)} async-done(((bf16[2048,256]{1,0:T(8,128)(2,1)}), bf16[2048,2048]{1,0:T(8,128)(2,1)}) %all-gather.22.cloned.1.call-update) | async-done | bytes 8388624 | tf_op jit(solution)/shard_map/all_gather | solution.py:134
  580.2 21.8 %multiply_convert_fusion = (bf16[1024,2048]{1,0:T(8,128)(2,1)}, bf16[1024,2048]{1,0:T(8,128)(2,1)}, bf16[1024,2048]{1,0:T(8,128)(2,1)}) fusion(f32[1024,2048]{1,0:T(8,128)} %fusion.77, f32[1024,2048]{1,0:T(8,128)} %fusion.78, bf16[1024,2048]{1,0:T(8,128)(2,1)} %all-gather.24.cloned.1.call-done, bf16[2048,2048]{1,0:T(8,128)(2,1)} %all-gather.22.cloned.1.call-done), kind=kOutput, calls=%fused_computation.69 | convolution fusion | flops 8623489024 | bytes 41943040 | tf_op jit(solution)/shard_map/rd,fd->rf/dot_general | solution.py:147
  602.0 12.9 fusion.79
  614.9 12.9 add_convert_fusion.1
  627.9 76.9 %reduce-scatter.16.cloned.1.call-done = bf16[256,2048]{1,0:T(8,128)(2,1)} async-done(((bf16[1024,2048]{1,0:T(8,128)(2,1)}), bf16[256,2048]{1,0:T(8,128)(2,1)}) %reduce-scatter.16.cloned.1.call-update) | async-done | bytes 1048592 | tf_op jit(solution)/shard_map/reduce_scatter | solution.py:155
  707.6 3.2 fusion.74
  710.8 14.4 %convolution_convert_fusion.1 = bf16[2048,2048]{1,0:T(8,128)(2,1)} fusion(bf16[1024,2048]{1,0:T(8,128)(2,1)} %all-gather.16.cloned.1.call-done, bf16[1024,2048]{1,0:T(8,128)(2,1)} %get-tuple-element.389), kind=kOutput, calls=%fused_computation.74 | convolution fusion | flops 8594128896 | bytes 16777216 | tf_op jit(solution)/shard_map/rd,rf->df/dot_general | solution.py:153
  725.3 14.1 %convolution_convert_fusion.2 = bf16[2048,2048]{1,0:T(8,128)(2,1)} fusion(bf16[1024,2048]{1,0:T(8,128)(2,1)} %all-gather.16.cloned.1.call-done, bf16[1024,2048]{1,0:T(8,128)(2,1)} %get-tuple-element.390), kind=kOutput, calls=%fused_computation.75 | convolution fusion | flops 8594128896 | bytes 16777216 | tf_op jit(solution)/shard_map/rd,rf->df/dot_general | solution.py:152
  739.5 14.1 %convolution_convert_fusion = bf16[2048,2048]{1,0:T(8,128)(2,1)} fusion(bf16[1024,2048]{1,0:T(8,128)(2,1)} %get-tuple-element.391, bf16[1024,2048]{1,0:T(8,128)(2,1)} %all-gather.24.cloned.1.call-done), kind=kOutput, calls=%fused_computation.73 | convolution fusion | flops 8594128896 | bytes 16777216 | tf_op jit(solution)/shard_map/rf,rd->fd/dot_general | solution.py:154
  753.7 38.5 %all-gather.26.cloned.1.call-done = bf16[1024,2048]{1,0:T(8,128)(2,1)} async-done(((bf16[256,2048]{1,0:T(8,128)(2,1)}), bf16[1024,2048]{1,0:T(8,128)(2,1)}) %all-gather.26.cloned.1.call-update) | async-done | bytes 4194320 | tf_op jit(solution)/shard_map/all_gather | solution.py:167
  792.2 5.5 convolution_convert_fusion.9
  797.7 133.2 %while.33 = (s32[]{:T(128)}, f32[1024,2,64]{0,2,1:T(8,128)}, f32[1024,2,64]{0,2,1:T(8,128)}, f32[2,512,2,4,64]{1,0,4,3,2:T(2,128)}, s32[2]{0:T(128)S(1)}, /*inde...) while((s32[]{:T(128)}, f32[1024,2,64]{0,2,1:T(8,128)}, ...), condition=%wide.region_12.13_spmd.clone, body=%wide.region_10.12_spmd.clone.sunk | while | flops 2749755904 | bytes 184482448 | solution.py:204
  802.5 3.6 fusion.159
  806.1 5.3 fusion.164
  811.4 11.0 fusion.161
  822.3 8.5 fusion.162
  830.8 3.3 copy-done
  836.6 6.1 fusion.165
  843.8 19.7 %dynamic_update_slice.31 = f32[2,512,2,4,64]{1,0,4,3,2:T(2,128)} dynamic-update-slice(f32[2,512,2,4,64]{1,0,4,3,2:T(2,128)} %get-tuple-element.599, f32[1,512,2,4,64]{1,0,4,3,2:T(1,128)S(1)} %copy.49, s32[]{:T(128)S(6)} %copy.66, s32[]{:T(128)} %constant.161.clone.1..sunk.1, s32[]{:T(128)} %constant.161.clone.1..sunk.1, s32[]{:T(128)} %constant.161.clone.1..sunk.1, s32[]{:T(128)} %constant.161.clone.1..sunk.1) | dynamic-update-slice | bytes 2097156 | tf_op jit(solution)/shard_map/while/body/jit(dynamic_update_index_in_dim)/dynamic_update_slice | solution.py:204
  868.0 3.5 fusion.159
  871.5 6.3 fusion.164
  877.8 11.1 fusion.161
  889.0 9.0 fusion.162
  898.0 3.3 copy-done
  903.7 6.2 fusion.165
  911.0 19.7 %dynamic_update_slice.31 = f32[2,512,2,4,64]{1,0,4,3,2:T(2,128)} dynamic-update-slice(f32[2,512,2,4,64]{1,0,4,3,2:T(2,128)} %get-tuple-element.599, f32[1,512,2,4,64]{1,0,4,3,2:T(1,128)S(1)} %copy.49, s32[]{:T(128)S(6)} %copy.66, s32[]{:T(128)} %constant.161.clone.1..sunk.1, s32[]{:T(128)} %constant.161.clone.1..sunk.1, s32[]{:T(128)} %constant.161.clone.1..sunk.1, s32[]{:T(128)} %constant.161.clone.1..sunk.1) | dynamic-update-slice | bytes 2097156 | tf_op jit(solution)/shard_map/while/body/jit(dynamic_update_index_in_dim)/dynamic_update_slice | solution.py:204
  932.1 4.3 convolution_convert_fusion.7
  936.6 4.5 convolution_convert_fusion.8
  941.2 5.9 convolution_convert_fusion.5
  947.2 3.1 reshape.216
  953.1 3.8 convolution_convert_fusion.6
  961.8 3.4 add_convert_fusion
  965.3 13.9 %convolution_convert_fusion.3 = bf16[1024,2048]{1,0:T(8,128)(2,1)} fusion(bf16[1024,2048]{1,0:T(8,128)(2,1)} %get-tuple-element.391, bf16[2048,2048]{1,0:T(8,128)(2,1)} %all-gather.22.cloned.1.call-done), kind=kOutput, calls=%fused_computation.81 | convolution fusion | flops 8592031744 | bytes 16777216 | tf_op jit(solution)/shard_map/dot_general | solution.py:140
  982.0 2.9 convert_element_type.191
  984.9 30.2 %reduce-scatter.32.cloned.1.call-done = bf16[2048,256]{1,0:T(8,128)(2,1)} async-done(((bf16[2048,2048]{1,0:T(8,128)(2,1)}), bf16[2048,256]{1,0:T(8,128)(2,1)}) %reduce-scatter.32.cloned.1.call-update) | async-done | bytes 1048592 | tf_op jit(solution)/shard_map/reduce_scatter | solution.py:250
  1017.9 35.0 %reduce-scatter.24.cloned.1.call-done = bf16[256,128]{1,0:T(8,128)(2,1)} async-done(((bf16[2048,128]{1,0:T(8,128)(2,1)}), bf16[256,128]{1,0:T(8,128)(2,1)}) %reduce-scatter.24.cloned.1.call-update) | async-done | bytes 65552 | tf_op jit(solution)/shard_map/reduce_scatter | solution.py:238
  1054.3 36.1 %reduce-scatter.22.cloned.1.call-done = bf16[256,128]{1,0:T(8,128)(2,1)} async-done(((bf16[2048,128]{1,0:T(8,128)(2,1)}), bf16[256,128]{1,0:T(8,128)(2,1)}) %reduce-scatter.22.cloned.1.call-update) | async-done | bytes 65552 | tf_op jit(solution)/shard_map/reduce_scatter | solution.py:235
  1092.0 42.8 %reduce-scatter.26.cloned.1.call-done = bf16[512,256]{1,0:T(8,128)(2,1)} async-done(((bf16[512,2048]{1,0:T(8,128)(2,1)}), bf16[512,256]{1,0:T(8,128)(2,1)}) %reduce-scatter.26.cloned.1.call-update) | async-done | bytes 262160 | tf_op jit(solution)/shard_map/reduce_scatter | solution.py:241
  1136.5 43.1 %reduce-scatter.20.cloned.1.call-done = bf16[256,512]{1,0:T(8,128)(2,1)} async-done(((bf16[2048,512]{1,0:T(8,128)(2,1)}), bf16[256,512]{1,0:T(8,128)(2,1)}) %reduce-scatter.20.cloned.1.call-update) | async-done | bytes 262160 | tf_op jit(solution)/shard_map/reduce_scatter | solution.py:232
  1181.4 77.3 %reduce-scatter.18.cloned.1.call-done = bf16[256,2048]{1,0:T(8,128)(2,1)} async-done(((bf16[1024,2048]{1,0:T(8,128)(2,1)}), bf16[256,2048]{1,0:T(8,128)(2,1)}) %reduce-scatter.18.cloned.1.call-update) | async-done | bytes 1048592 | tf_op jit(solution)/shard_map/reduce_scatter | solution.py:217
  1261.0 45.8 %all-reduce.4 = (f32[2048]{0:T(1024)}, f32[2048]{0:T(1024)}) all-reduce(f32[2048]{0:T(1024)S(1)} %get-tuple-element.341, f32[2048]{0:T(1024)S(1)} %copy-done.35), channel_id=1, replica_groups=mesh['dp'=8,'tensor'=4] {'dp','tensor'}, use_global_device_ids=true, to_apply=%region_16.17 | all-reduce | flops 4096 | bytes 32768 | tf_op jit(solution)/shard_map/psum | solution.py:230
  1306.8 32.4 %reduce-scatter.14.cloned.1.call-done = bf16[256,2048]{1,0:T(8,128)(2,1)} async-done(((bf16[1024,2048]{1,0:T(8,128)(2,1)}), bf16[256,2048]{1,0:T(8,128)(2,1)}) %reduce-scatter.14.cloned.1.call-update) | async-done | bytes 1048592 | tf_op jit(solution)/shard_map/reduce_scatter | solution.py:139
  1339.3 5.1 fusion.69
  (217 shorter events, 61.4 us)
Async XLA Ops:
  7.2 6.8 copy-start.44
  7.2 6.8 copy-start.33
  7.2 18.2 %copy-start.34 = (bf16[256,128]{1,0:T(8,128)(2,1)S(1)}, bf16[256,128]{1,0:T(8,128)(2,1)}, u32[]{:S(2)}) copy-start(bf16[256,128]{1,0:T(8,128)(2,1)} %param.23) | copy-start | bytes 196612
  7.2 88.8 %all-gather.10.cloned.1.call-start = ((), (), s32[]{:S(2)}) async-start(), calls=%async_computation.11 | async-start | bytes 5242880 | tf_op jit(solution)/shard_map/all_gather | solution.py:66
  12.4 111.8 %all-gather.12.cloned.1.call-start = ((), (), s32[]{:S(2)}) async-start(), calls=%async_computation.12 | async-start | bytes 2359296 | tf_op jit(solution)/shard_map/all_gather | solution.py:68
  13.2 150.5 %all-gather.14.cloned.1.call-start = ((), (), s32[]{:S(2)}) async-start(), calls=%async_computation.13 | async-start | bytes 2359296 | tf_op jit(solution)/shard_map/all_gather | solution.py:71
  13.9 233.7 %reduce-scatter.12.cloned.1.call-start = ((), (), s32[]{:S(2)}) async-start(), calls=%async_computation.14 | async-start | bytes 5242880 | tf_op jit(solution)/shard_map/reduce_scatter | solution.py:122
  25.4 104.1 %copy-start.21 = (bf16[2048,128]{1,0:T(8,128)(2,1)}, bf16[2048,128]{1,0:T(8,128)(2,1)S(1)}, u32[]{:S(2)}) copy-start(bf16[2048,128]{1,0:T(8,128)(2,1)S(1)} %all_gather.35) | copy-start | bytes 1572868
  35.2 94.8 %copy-start.19 = (bf16[2048,128]{1,0:T(8,128)(2,1)}, bf16[2048,128]{1,0:T(8,128)(2,1)S(1)}, u32[]{:S(2)}) copy-start(bf16[2048,128]{1,0:T(8,128)(2,1)S(1)} %all_gather.36) | copy-start | bytes 1572868
  35.7 93.8 %copy-start.24 = (f32[1024,32]{0,1:T(8,128)}, f32[1024,32]{0,1:T(8,128)S(1)}, u32[]{:S(2)}) copy-start(f32[1024,32]{0,1:T(8,128)S(1)} %get-tuple-element.402) | copy-start | bytes 393220
  35.7 93.8 %copy-start.26 = (f32[1024,32]{0,1:T(8,128)}, f32[1024,32]{0,1:T(8,128)S(1)}, u32[]{:S(2)}) copy-start(f32[1024,32]{0,1:T(8,128)S(1)} %get-tuple-element.403) | copy-start | bytes 393220
  163.7 6.9 copy-start.1
  163.7 6.9 copy-start.3
  163.7 6.9 copy-start.14
  170.6 77.0 %copy-start.5 = (bf16[256,2048]{1,0:T(8,128)(2,1)S(1)}, bf16[256,2048]{1,0:T(8,128)(2,1)}, u32[]{:S(2)}) copy-start(bf16[256,2048]{1,0:T(8,128)(2,1)} %param.17) | copy-start | bytes 3145732
  170.6 78.6 %copy-start.30 = (f32[2048]{0:T(1024)S(1)}, f32[2048]{0:T(1024)}, u32[]{:S(2)}) copy-start(f32[2048]{0:T(1024)} %param.25) | copy-start | bytes 24580
  170.7 133.5 %all-gather.20.cloned.1.call-start = ((), (), s32[]{:S(2)}) async-start(), calls=%async_computation.17 | async-start | bytes 9437184 | tf_op jit(solution)/shard_map/all_gather | solution.py:133
  171.2 215.6 %all-gather.16.cloned.1.call-start = ((), (), s32[]{:S(2)}) async-start(), calls=%async_computation.15 | async-start | bytes 5242880 | tf_op jit(solution)/shard_map/all_gather | solution.py:130
  249.2 458.3 %copy-start.36 = (f32[256]{0:T(256)}, f32[256]{0:T(256)S(1)}, u32[]{:S(2)}) copy-start(f32[256]{0:T(256)S(1)} %fusion.73) | copy-start | bytes 3076
  251.9 189.7 %all-gather.18.cloned.1.call-start = ((), (), s32[]{:S(2)}) async-start(), calls=%async_computation.16 | async-start | bytes 9437184 | tf_op jit(solution)/shard_map/all_gather | solution.py:132
  252.6 271.3 %all-gather.24.cloned.1.call-start = ((), (), s32[]{:S(2)}) async-start(), calls=%async_computation.20 | async-start | bytes 5242880 | tf_op jit(solution)/shard_map/all_gather | solution.py:146
  253.4 326.8 %all-gather.22.cloned.1.call-start = ((), (), s32[]{:S(2)}) async-start(), calls=%async_computation.18 | async-start | bytes 9437184 | tf_op jit(solution)/shard_map/all_gather | solution.py:134
  254.1 450.7 %reduce-scatter.16.cloned.1.call-start = ((), (), s32[]{:S(2)}) async-start(), calls=%async_computation.21 | async-start | bytes 5242880 | tf_op jit(solution)/shard_map/reduce_scatter | solution.py:155
  602.0 12.9 copy-start.48
  627.8 77.0 %copy-start.10 = (bf16[256,2048]{1,0:T(8,128)(2,1)S(1)}, bf16[256,2048]{1,0:T(8,128)(2,1)}, u32[]{:S(2)}) copy-start(bf16[256,2048]{1,0:T(8,128)(2,1)} %reduce-scatter.12.cloned.1.call-done) | copy-start | bytes 3145732
  627.8 79.8 %copy-start.16 = (bf16[256,2048]{1,0:T(8,128)(2,1)S(1)}, bf16[256,2048]{1,0:T(8,128)(2,1)}, u32[]{:S(2)}) copy-start(bf16[256,2048]{1,0:T(8,128)(2,1)} %param.29) | copy-start | bytes 3145732
  627.8 164.4 %all-gather.26.cloned.1.call-start = ((), (), s32[]{:S(2)}) async-start(), calls=%async_computation.22 | async-start | bytes 5242880 | tf_op jit(solution)/shard_map/all_gather | solution.py:167
  707.6 17.7 %copy-start.40 = (f32[256]{0:T(256)}, f32[256]{0:T(256)S(1)}, u32[]{:S(2)}) copy-start(f32[256]{0:T(256)S(1)} %multiply_multiply_fusion.1) | copy-start | bytes 3076
  710.8 268.4 %reduce-scatter.30.cloned.1.call-start = ((), (), s32[]{:S(2)}) async-start(), calls=%async_computation.29 | async-start | bytes 9437184 | tf_op jit(solution)/shard_map/reduce_scatter | solution.py:247
  725.3 256.7 %reduce-scatter.28.cloned.1.call-start = ((), (), s32[]{:S(2)}) async-start(), calls=%async_computation.28 | async-start | bytes 9437184 | tf_op jit(solution)/shard_map/reduce_scatter | solution.py:244
  739.5 275.7 %reduce-scatter.32.cloned.1.call-start = ((), (), s32[]{:S(2)}) async-start(), calls=%async_computation.30 | async-start | bytes 9437184 | tf_op jit(solution)/shard_map/reduce_scatter | solution.py:250
  753.6 38.6 %copy-start.46 = (bf16[512,2048]{1,0:T(8,128)(2,1)S(1)}, bf16[512,2048]{1,0:T(8,128)(2,1)}, u32[]{:S(2)}) copy-start(bf16[512,2048]{1,0:T(8,128)(2,1)} %all-gather.14.cloned.1.call-done) | copy-start | bytes 6291460
  753.6 44.1 %copy-start.4 = (bf16[1024,2,64]{0,2,1:T(8,128)(2,1)S(1)}, bf16[1024,2,64]{0,2,1:T(8,128)(2,1)}, u32[]{:S(2)}) copy-start(bf16[1024,2,64]{0,2,1:T(8,128)(2,1)} %copy-done.3) | copy-start | bytes 786436
  753.6 44.1 %copy-start.15 = (bf16[1024,2,64]{0,2,1:T(8,128)(2,1)S(1)}, bf16[1024,2,64]{0,2,1:T(8,128)(2,1)}, u32[]{:S(2)}) copy-start(bf16[1024,2,64]{0,2,1:T(8,128)(2,1)} %copy-done.14) | copy-start | bytes 786436
  753.7 44.0 %copy-start.29 = (s32[1024]{0:T(1024)S(1)}, s32[1024]{0:T(1024)}, u32[]{:S(2)}) copy-start(s32[1024]{0:T(1024)} %param.18) | copy-start | bytes 12292
  753.7 299.1 %reduce-scatter.24.cloned.1.call-start = ((), (), s32[]{:S(2)}) async-start(), calls=%async_computation.26 | async-start | bytes 589824 | tf_op jit(solution)/shard_map/reduce_scatter | solution.py:238
  801.9 4.1 copy-start.23
  802.4 3.6 copy-start.18
  822.3 11.8 copy-start.2
  822.3 11.8 copy-start.7
  867.5 4.0 copy-start.23
  868.0 3.5 copy-start.18
  889.0 12.3 copy-start.2
  889.0 12.3 copy-start.7
  930.9 5.6 copy-start.9
  930.9 5.6 copy-start.25
  930.9 5.6 copy-start.27
  936.4 4.8 copy-start.47
  936.4 154.0 %reduce-scatter.22.cloned.1.call-start = ((), (), s32[]{:S(2)}) async-start(), calls=%async_computation.25 | async-start | bytes 589824 | tf_op jit(solution)/shard_map/reduce_scatter | solution.py:235
  941.2 193.6 %reduce-scatter.26.cloned.1.call-start = ((), (), s32[]{:S(2)}) async-start(), calls=%async_computation.27 | async-start | bytes 2359296 | tf_op jit(solution)/shard_map/reduce_scatter | solution.py:241
  947.1 232.5 %reduce-scatter.20.cloned.1.call-start = ((), (), s32[]{:S(2)}) async-start(), calls=%async_computation.24 | async-start | bytes 2359296 | tf_op jit(solution)/shard_map/reduce_scatter | solution.py:232
  953.1 4.3 copy-start.22
  956.9 301.8 %reduce-scatter.18.cloned.1.call-start = ((), (), s32[]{:S(2)}) async-start(), calls=%async_computation.23 | async-start | bytes 5242880 | tf_op jit(solution)/shard_map/reduce_scatter | solution.py:217
  965.2 374.0 %reduce-scatter.14.cloned.1.call-start = ((), (), s32[]{:S(2)}) async-start(), calls=%async_computation.19 | async-start | bytes 5242880 | tf_op jit(solution)/shard_map/reduce_scatter | solution.py:139
  982.0 276.7 %copy-start.6 = (bf16[256,2048]{1,0:T(8,128)(2,1)S(1)}, bf16[256,2048]{1,0:T(8,128)(2,1)}, u32[]{:S(2)}) copy-start(bf16[256,2048]{1,0:T(8,128)(2,1)} %param.17) | copy-start | bytes 3145732
  982.0 276.7 %copy-start.32 = (f32[2048]{0:T(1024)S(1)}, f32[2048]{0:T(1024)}, u32[]{:S(2)}) copy-start(f32[2048]{0:T(1024)} %param.20) | copy-start | bytes 24580
  982.0 276.7 %copy-start.39 = (f32[256]{0:T(256)S(1)}, f32[256]{0:T(256)}, u32[]{:S(2)}) copy-start(f32[256]{0:T(256)} %copy-done.38) | copy-start | bytes 3076
  984.9 276.1 %copy-start.35 = (f32[2048]{0:T(1024)S(1)}, f32[2048]{0:T(1024)}, u32[]{:S(2)}) copy-start(f32[2048]{0:T(1024)} %get-tuple-element.339) | copy-start | bytes 24580
  984.9 321.9 %copy-start.43 = (f32[256]{0:T(256)S(1)}, f32[256]{0:T(256)}, u32[]{:S(2)}) copy-start(f32[256]{0:T(256)} %copy-done.42) | copy-start | bytes 3076
  984.9 354.3 %copy-start.11 = (bf16[256,2048]{1,0:T(8,128)(2,1)S(1)}, bf16[256,2048]{1,0:T(8,128)(2,1)}, u32[]{:S(2)}) copy-start(bf16[256,2048]{1,0:T(8,128)(2,1)} %reduce-scatter.12.cloned.1.call-done) | copy-start | bytes 3145732
  984.9 354.3 %copy-start.17 = (bf16[256,2048]{1,0:T(8,128)(2,1)S(1)}, bf16[256,2048]{1,0:T(8,128)(2,1)}, u32[]{:S(2)}) copy-start(bf16[256,2048]{1,0:T(8,128)(2,1)} %param.29) | copy-start | bytes 3145732
  984.9 354.3 %copy-start.31 = (f32[2048]{0:T(1024)S(1)}, f32[2048]{0:T(1024)}, u32[]{:S(2)}) copy-start(f32[2048]{0:T(1024)} %param.25) | copy-start | bytes 24580
  984.9 354.3 %copy-start.37 = (f32[256]{0:T(256)S(1)}, f32[256]{0:T(256)}, u32[]{:S(2)}) copy-start(f32[256]{0:T(256)} %copy-done.36) | copy-start | bytes 3076
  984.9 354.3 %copy-start.41 = (f32[256]{0:T(256)S(1)}, f32[256]{0:T(256)}, u32[]{:S(2)}) copy-start(f32[256]{0:T(256)} %copy-done.40) | copy-start | bytes 3076
  (11 other events, 22.1 us)
Sparse Core Ops, SparseCore 0:
  12.6 83.4 all-gather.9
  97.9 26.2 all-gather.11
  126.1 28.1 all-gather.13
  170.8 76.7 reduce-scatter.11
  249.3 54.7 all-gather.19
  306.1 80.7 all-gather.15
  388.8 52.7 all-gather.17
  443.1 80.7 all-gather.23
  525.8 54.3 all-gather.21
  627.9 76.7 reduce-scatter.15
  710.9 81.2 all-gather.25
  795.5 69.9 reduce-scatter.29
  869.0 71.4 reduce-scatter.27
  943.8 71.2 reduce-scatter.31
  1018.7 34.1 reduce-scatter.23
  1056.3 34.0 reduce-scatter.21
  1093.6 41.1 reduce-scatter.25
  1138.5 41.0 reduce-scatter.19
  1181.9 76.7 reduce-scatter.17
  1260.9 78.3 reduce-scatter.13
where the time goes:
time: 1360 us; the launch traced here: 1350 us
  waiting for transfers between devices  874 us (64%)
  matrix products  253 us (19%)
  other arithmetic  68.7 us (5%)
  blocking collectives  67 us (5%)
  local copies, waits for them, and re-layouts  65 us (5%)
  between operations  15.1 us (1%)
    all_gather x1, waiting for transfers between devices, local(): normed_mid = lax.all_gather(normed_mid_local, 'tensor', axis=0, tiled=True)  82.8 us
    reduce_scatter x1, waiting for transfers between devices, local(): lax.psum_scatter((jnp.einsum('rc,dc->rd', query_rows, query_all, preferre...  77.3 us
    reduce_scatter x1, waiting for transfers between devices, local(): lax.psum_scatter((jnp.einsum('rf,df->rd', d_gate, gate_all, preferred_ele...  76.9 us
    reduce_scatter x1, waiting for transfers between devices, local(): lax.psum_scatter(jnp.dot(context, out_all, preferred_element_type=jnp.flo...  76.3 us
    all_gather x1, waiting for transfers between devices, local(): cot_all = lax.all_gather(cotangent, 'tensor', axis=0, tiled=True)  67.9 us
    all_gather x1, waiting for transfers between devices, local(): normed_in = lax.all_gather(normed_local, 'tensor', axis=0, tiled=True)  60.3 us
    all_gather x1, waiting for transfers between devices, local(): lax.all_gather(w_down, 'dp', axis=1, tiled=True)  56.3 us
    all_gather x1, waiting for transfers between devices, local(): lax.all_gather(w_up, 'dp', axis=0, tiled=True)  50 us
  transfers between devices with their start and end apart: 20, of which 17 were waited for; matrix products, arithmetic and copies ran while one was open for 22% of the time, Pallas kernels for 0%

commit v1 on v0

--- a/solution.py
+++ b/solution.py
@@ -1,14 +1,38 @@
+import functools
 from functools import partial
 import math
 import jax
 import jax.numpy as jnp
 from jax import lax
 from jax.sharding import PartitionSpec as P
+from jax.lax import axis_index, axis_size, ppermute
 
 QH = 32
 KVH = 8
 HD = 64
 LEN = 1024
+
+
+def apply_the_matrix(view, row_axis):
+    cores_n = axis_size(row_axis)
+    x_now = range(cores_n)
+    w1 = range(cores_n)
+    cards = list(map(lambda hop_no: (hop_no, (hop_no + 1) % cores_n), x_now))
+    slots = list(map(lambda hop_no: (hop_no, (hop_no - 1) % cores_n), w1))
+    tile_out, known = ([view], [view])
+    for _ in range(cores_n // 2):
+        opened = ppermute(tile_out[-1], row_axis, cards)
+        tile_out.append(opened)
+    for _ in range((cores_n - 1) // 2):
+        fresh = ppermute(known[-1], row_axis, slots)
+        known.append(fresh)
+    u_next = jnp.concatenate([*tile_out[::-1], *known[1:]], axis=0)
+    mid_arr = axis_index(row_axis)
+    y = jnp.roll(u_next, (mid_arr - cores_n // 2) * view.shape[0], axis=0)
+    return y
+
+
+_make_array = functools.partial(apply_the_matrix, row_axis="tensor")
 
 
 def rms_scale(values, norm_gain):
@@ -164,7 +188,7 @@
     mid_back = jax.vjp(rms_scale, middle, norm_mlp)[1]
     d_middle_norm, mlp_gain_part = mid_back(d_normed_mid)
     d_middle = cotangent.astype(jnp.float32) + d_middle_norm
-    d_branch = lax.all_gather(d_middle.astype(jnp.bfloat16), "tensor", axis=0, tiled=True)
+    d_branch = _make_array(d_middle.astype(jnp.bfloat16))
     out_part = jnp.einsum("rc,rd->cd", context, d_branch, preferred_element_type=jnp.float32)
     d_context = jnp.einsum(
         "rd,cd->rc", d_branch, out_all, preferred_element_type=jnp.float32

time: 1360 us -> 1500 us (1.10)
  waiting for transfers between devices: 874 us -> 1000 us
    reduce_scatter x1, waiting for transfers between devices: 0.01 us -> 72 us  [local(): lax.psum_scatter(gate_part.astype(jnp.bfloat16), 'dp', scatter_dimension=...]
    ppermute x0 -> x3, waiting for transfers between devices: none -> 66.4 us  [the longest x2 49.1 us: apply_the_matrix(): opened = ppermute(tile_out[-1], row_axis, cards)]
    reduce_scatter x1, waiting for transfers between devices: 0.02 us -> 58 us  [local(): lax.psum_scatter(up_part.astype(jnp.bfloat16), 'dp', scatter_dimension=0,...]
    reduce_scatter x1, waiting for transfers between devices: 30.2 us -> 71.8 us  [local(): lax.psum_scatter(down_part.astype(jnp.bfloat16), 'dp', scatter_dimension=...]
    all_gather x1 -> x0, waiting for transfers between devices: 38.5 us -> none  [local(): lax.all_gather(d_middle.astype(jnp.bfloat16), 'tensor', axis=0, tiled=True)]
    reduce_scatter x1, waiting for transfers between devices: 36.1 us -> 0.01 us  [local(): lax.psum_scatter(key_part.astype(jnp.bfloat16), 'dp', scatter_dimension=0...]
    reduce_scatter x1, waiting for transfers between devices: 35 us -> 0.02 us  [local(): lax.psum_scatter(value_part.astype(jnp.bfloat16), 'dp', scatter_dimension...]
  transfers between devices with their start and end apart: 20 -> 22, of which waited for: 17 -> 19; matrix products, arithmetic and copies ran while one was open for 22% -> 12% of each run, Pallas kernels for 0% -> 0%
where the time goes in v1:
time: 1500 us; the launch traced here: 1490 us
  waiting for transfers between devices  1000 us (67%)
  matrix products  255 us (17%)
  other arithmetic  69.7 us (5%)
  blocking collectives  67.2 us (4%)
  local copies, waits for them, and re-layouts  63.3 us (4%)
  between operations  15.1 us (1%)
    all_gather x1, waiting for transfers between devices, local(): normed_mid = lax.all_gather(normed_mid_local, 'tensor', axis=0, tiled=True)  82.8 us
    reduce_scatter x1, waiting for transfers between devices, local(): lax.psum_scatter((jnp.einsum('rc,dc->rd', query_rows, query_all, preferre...  77.2 us
    reduce_scatter x1, waiting for transfers between devices, local(): lax.psum_scatter((jnp.einsum('rf,df->rd', d_gate, gate_all, preferred_ele...  76.9 us
    reduce_scatter x1, waiting for transfers between devices, local(): lax.psum_scatter(jnp.dot(context, out_all, preferred_element_type=jnp.flo...  76.3 us
    reduce_scatter x1, waiting for transfers between devices, local(): lax.psum_scatter(gate_part.astype(jnp.bfloat16), 'dp', scatter_dimension=...  72 us
    reduce_scatter x1, waiting for transfers between devices, local(): lax.psum_scatter(down_part.astype(jnp.bfloat16), 'dp', scatter_dimension=...  71.8 us
    all_gather x1, waiting for transfers between devices, local(): cot_all = lax.all_gather(cotangent, 'tensor', axis=0, tiled=True)  67.8 us
    all_gather x1, waiting for transfers between devices, local(): normed_in = lax.all_gather(normed_local, 'tensor', axis=0, tiled=True)  60.3 us
  transfers between devices with their start and end apart: 22, of which 19 were waited for; matrix products, arithmetic and copies ran while one was open for 12% of the time, Pallas kernels for 0%

profile of v1, /device:TPU:0, one launch (start us, length us, event | category | flops | bytes accessed | tf_op | source)
XLA Modules:
  0.0 1485.3 jit_solution(5428923198007650896)
XLA Ops:
  12.9 11.3 all_gather.32
  24.3 9.8 all_gather.33
  34.7 60.3 %all-gather.9.cloned.1.call-done = bf16[1024,2048]{1,0:T(8,128)(2,1)} async-done(((bf16[256,2048]{1,0:T(8,128)(2,1)}), bf16[1024,2048]{1,0:T(8,128)(2,1)}) %all-gather.9.cloned.1.call-update) | async-done | bytes 4194320 | tf_op jit(solution)/shard_map/all_gather | solution.py:90
  94.9 3.7 fusion.88
  98.7 24.4 %all-gather.11.cloned.1.call-done = bf16[2048,512]{1,0:T(8,128)(2,1)} async-done(((bf16[256,512]{1,0:T(8,128)(2,1)}), bf16[2048,512]{1,0:T(8,128)(2,1)}) %all-gather.11.cloned.1.call-update) | async-done | bytes 2097168 | tf_op jit(solution)/shard_map/all_gather | solution.py:92
  123.1 5.2 fusion.87
  132.5 30.9 %while.32 = (s32[]{:T(128)}, bf16[2,512,512]{2,1,0:T(8,128)(2,1)S(1)}, f32[2,2,4,512,1]{3,2,1,4,0:T(4,128)}, s32[2]{0:T(128)S(1)}, s32[1024]{0:T(1024)S(1)}, /*i...) while((s32[]{:T(128)}, ...), condition=%wide.region_4.5_spmd.clone, body=%wide.region_1.4_spmd.clone.sunk | while | flops 1121710592 | bytes 56244616 | solution.py:144
  134.6 3.9 bitcast_reduce_fusion.2
  138.5 4.4 fusion.159
  143.4 4.4 fusion.160
  149.9 3.9 bitcast_reduce_fusion.2
  153.8 4.4 fusion.159
  158.8 4.4 fusion.160
  163.5 6.3 convolution_convert_fusion.4
  170.5 76.3 %reduce-scatter.12.cloned.1.call-done = bf16[256,2048]{1,0:T(8,128)(2,1)} async-done(((bf16[1024,2048]{1,0:T(8,128)(2,1)}), bf16[256,2048]{1,0:T(8,128)(2,1)}) %reduce-scatter.12.cloned.1.call-update) | async-done | bytes 1048592 | tf_op jit(solution)/shard_map/reduce_scatter | solution.py:146
  253.3 50.0 %all-gather.19.cloned.1.call-done = bf16[2048,2048]{1,0:T(8,128)(2,1)} async-done(((bf16[256,2048]{1,0:T(8,128)(2,1)}), bf16[2048,2048]{1,0:T(8,128)(2,1)}) %all-gather.19.cloned.1.call-update) | async-done | bytes 8388624 | tf_op jit(solution)/shard_map/all_gather | solution.py:157
  303.3 82.8 %all-gather.15.cloned.1.call-done = bf16[1024,2048]{1,0:T(8,128)(2,1)} async-done(((bf16[256,2048]{1,0:T(8,128)(2,1)}), bf16[1024,2048]{1,0:T(8,128)(2,1)}) %all-gather.15.cloned.1.call-update) | async-done | bytes 4194320 | tf_op jit(solution)/shard_map/all_gather | solution.py:154
  386.1 14.9 %fusion.90 = f32[1024,2048]{1,0:T(8,128)} fusion(bf16[1024,2048]{1,0:T(8,128)(2,1)} %all-gather.15.cloned.1.call-done, bf16[2048,2048]{1,0:T(8,128)(2,1)} %all-gather.19.cloned.1.call-done), kind=kOutput, calls=%fused_computation.149 | convolution fusion | flops 8589934592 | bytes 20971520 | tf_op jit(solution)/shard_map/dot_general | solution.py:161
  401.0 39.8 %all-gather.17.cloned.1.call-done = bf16[2048,2048]{1,0:T(8,128)(2,1)} async-done(((bf16[256,2048]{1,0:T(8,128)(2,1)}), bf16[2048,2048]{1,0:T(8,128)(2,1)}) %all-gather.17.cloned.1.call-update) | async-done | bytes 8388624 | tf_op jit(solution)/shard_map/all_gather | solution.py:156
  440.7 14.5 fusion.89
  455.3 67.8 %all-gather.23.cloned.1.call-done = bf16[1024,2048]{1,0:T(8,128)(2,1)} async-done(((bf16[256,2048]{1,0:T(8,128)(2,1)}), bf16[1024,2048]{1,0:T(8,128)(2,1)}) %all-gather.23.cloned.1.call-update) | async-done | bytes 4194320 | tf_op jit(solution)/shard_map/all_gather | solution.py:170
  523.1 56.3 %all-gather.21.cloned.1.call-done = bf16[2048,2048]{1,0:T(8,128)(2,1)} async-done(((bf16[2048,256]{1,0:T(8,128)(2,1)}), bf16[2048,2048]{1,0:T(8,128)(2,1)}) %all-gather.21.cloned.1.call-update) | async-done | bytes 8388624 | tf_op jit(solution)/shard_map/all_gather | solution.py:158
  579.3 21.7 %multiply_convert_fusion = (bf16[1024,2048]{1,0:T(8,128)(2,1)}, bf16[1024,2048]{1,0:T(8,128)(2,1)}, bf16[1024,2048]{1,0:T(8,128)(2,1)}) fusion(f32[1024,2048]{1,0:T(8,128)} %fusion.89, f32[1024,2048]{1,0:T(8,128)} %fusion.90, bf16[1024,2048]{1,0:T(8,128)(2,1)} %all-gather.23.cloned.1.call-done, bf16[2048,2048]{1,0:T(8,128)(2,1)} %all-gather.21.cloned.1.call-done), kind=kOutput, calls=%fused_computation.69 | convolution fusion | flops 8623489024 | bytes 41943040 | tf_op jit(solution)/shard_map/rd,fd->rf/dot_general | solution.py:171
  601.1 12.9 fusion.91
  614.0 12.9 add_convert_fusion.1
  626.9 76.9 %reduce-scatter.16.cloned.1.call-done = bf16[256,2048]{1,0:T(8,128)(2,1)} async-done(((bf16[1024,2048]{1,0:T(8,128)(2,1)}), bf16[256,2048]{1,0:T(8,128)(2,1)}) %reduce-scatter.16.cloned.1.call-update) | async-done | bytes 1048592 | tf_op jit(solution)/shard_map/reduce_scatter | solution.py:179
  711.3 25.1 %collective-permute-done = bf16[256,2048]{1,0:T(8,128)(2,1)S(1)} collective-permute-done((bf16[256,2048]{1,0:T(8,128)(2,1)}, bf16[256,2048]{1,0:T(8,128)(2,1)S(1)}, u32[]{:S(2)}, u32[]{:S(2)}) %collective-permute-start) | collective-permute-done | bytes 1048608 | tf_op jit(solution)/shard_map/ppermute | solution.py:24
  736.4 3.8 collective-permute-start.2
  740.3 24.0 %collective-permute-done.1 = bf16[256,2048]{1,0:T(8,128)(2,1)S(1)} collective-permute-done((bf16[256,2048]{1,0:T(8,128)(2,1)S(1)}, bf16[256,2048]{1,0:T(8,128)(2,1)S(1)}, u32[]{:S(2)}, u32[]{:S(2)}) %collective-permute-start.1) | collective-permute-done | bytes 1048608 | tf_op jit(solution)/shard_map/ppermute | solution.py:24
  765.8 17.3 %collective-permute-done.2 = bf16[256,2048]{1,0:T(8,128)(2,1)S(1)} collective-permute-done((bf16[256,2048]{1,0:T(8,128)(2,1)}, bf16[256,2048]{1,0:T(8,128)(2,1)S(1)}, u32[]{:S(2)}, u32[]{:S(2)}) %collective-permute-start.2) | collective-permute-done | bytes 1048608 | tf_op jit(solution)/shard_map/ppermute | solution.py:27
  785.0 3.7 fusion.79
  788.7 133.4 %while.33 = (s32[]{:T(128)}, f32[1024,2,64]{0,2,1:T(8,128)}, f32[1024,2,64]{0,2,1:T(8,128)}, f32[2,512,2,4,64]{1,0,4,3,2:T(2,128)}, s32[2]{0:T(128)S(1)}, /*inde...) while((s32[]{:T(128)}, f32[1024,2,64]{0,2,1:T(8,128)}, ...), condition=%wide.region_12.13_spmd.clone, body=%wide.region_10.12_spmd.clone.sunk | while | flops 2749755904 | bytes 176093744 | solution.py:228
  793.7 3.5 fusion.169
  797.2 5.3 fusion.174
  802.5 10.9 fusion.171
  813.4 8.2 fusion.172
  824.8 3.5 fusion.173
  828.2 6.0 fusion.175
  835.4 19.6 %dynamic_update_slice.31 = f32[2,512,2,4,64]{1,0,4,3,2:T(2,128)} dynamic-update-slice(f32[2,512,2,4,64]{1,0,4,3,2:T(2,128)} %get-tuple-element.599, f32[1,512,2,4,64]{1,0,4,3,2:T(1,128)S(1)} %copy.49, s32[]{:T(128)S(6)} %copy.73, s32[]{:T(128)} %constant.185.clone.1..sunk.1, s32[]{:T(128)} %constant.185.clone.1..sunk.1, s32[]{:T(128)} %constant.185.clone.1..sunk.1, s32[]{:T(128)} %constant.185.clone.1..sunk.1) | dynamic-update-slice | bytes 2097156 | tf_op jit(solution)/shard_map/while/body/jit(dynamic_update_index_in_dim)/dynamic_update_slice | solution.py:228
  859.5 3.5 fusion.169
  863.0 6.3 fusion.174
  869.4 10.9 fusion.171
  880.2 8.2 fusion.172
  891.6 3.6 fusion.173
  895.3 6.0 fusion.175
  902.4 19.6 %dynamic_update_slice.31 = f32[2,512,2,4,64]{1,0,4,3,2:T(2,128)} dynamic-update-slice(f32[2,512,2,4,64]{1,0,4,3,2:T(2,128)} %get-tuple-element.599, f32[1,512,2,4,64]{1,0,4,3,2:T(1,128)S(1)} %copy.49, s32[]{:T(128)S(6)} %copy.73, s32[]{:T(128)} %constant.185.clone.1..sunk.1, s32[]{:T(128)} %constant.185.clone.1..sunk.1, s32[]{:T(128)} %constant.185.clone.1..sunk.1, s32[]{:T(128)} %constant.185.clone.1..sunk.1) | dynamic-update-slice | bytes 2097156 | tf_op jit(solution)/shard_map/while/body/jit(dynamic_update_index_in_dim)/dynamic_update_slice | solution.py:228
  923.3 4.3 convolution_convert_fusion.6
  928.8 4.3 convolution_convert_fusion.7
  933.2 14.1 convolution_convert_fusion.1
  947.4 14.1 convolution_convert_fusion.2
  961.5 14.3 convolution_convert_fusion
  977.1 5.9 fusion.64
  988.3 3.8 convolution_convert_fusion.5
  996.5 3.3 add_convert_fusion
  999.8 13.8 convolution_convert_fusion.3
  1016.8 58.0 %reduce-scatter.30.cloned.1.call-done = bf16[256,2048]{1,0:T(8,128)(2,1)} async-done(((bf16[2048,2048]{1,0:T(8,128)(2,1)}), bf16[256,2048]{1,0:T(8,128)(2,1)}) %reduce-scatter.30.cloned.1.call-update) | async-done | bytes 1048592 | tf_op jit(solution)/shard_map/reduce_scatter | solution.py:271
  1077.6 72.0 %reduce-scatter.28.cloned.1.call-done = bf16[256,2048]{1,0:T(8,128)(2,1)} async-done(((bf16[2048,2048]{1,0:T(8,128)(2,1)}), bf16[256,2048]{1,0:T(8,128)(2,1)}) %reduce-scatter.28.cloned.1.call-update) | async-done | bytes 1048592 | tf_op jit(solution)/shard_map/reduce_scatter | solution.py:268
  1152.5 71.8 %reduce-scatter.32.cloned.1.call-done = bf16[2048,256]{1,0:T(8,128)(2,1)} async-done(((bf16[2048,2048]{1,0:T(8,128)(2,1)}), bf16[2048,256]{1,0:T(8,128)(2,1)}) %reduce-scatter.32.cloned.1.call-update) | async-done | bytes 1048592 | tf_op jit(solution)/shard_map/reduce_scatter | solution.py:274
  1227.0 41.6 %reduce-scatter.26.cloned.1.call-done = bf16[512,256]{1,0:T(8,128)(2,1)} async-done(((bf16[512,2048]{1,0:T(8,128)(2,1)}), bf16[512,256]{1,0:T(8,128)(2,1)}) %reduce-scatter.26.cloned.1.call-update) | async-done | bytes 262160 | tf_op jit(solution)/shard_map/reduce_scatter | solution.py:265
  1270.4 43.1 %reduce-scatter.20.cloned.1.call-done = bf16[256,512]{1,0:T(8,128)(2,1)} async-done(((bf16[2048,512]{1,0:T(8,128)(2,1)}), bf16[256,512]{1,0:T(8,128)(2,1)}) %reduce-scatter.20.cloned.1.call-update) | async-done | bytes 262160 | tf_op jit(solution)/shard_map/reduce_scatter | solution.py:256
  1315.2 77.2 %reduce-scatter.18.cloned.1.call-done = bf16[256,2048]{1,0:T(8,128)(2,1)} async-done(((bf16[1024,2048]{1,0:T(8,128)(2,1)}), bf16[256,2048]{1,0:T(8,128)(2,1)}) %reduce-scatter.18.cloned.1.call-update) | async-done | bytes 1048592 | tf_op jit(solution)/shard_map/reduce_scatter | solution.py:241
  1394.7 46.0 %all-reduce.4 = (f32[2048]{0:T(1024)}, f32[2048]{0:T(1024)}) all-reduce(f32[2048]{0:T(1024)S(1)} %get-tuple-element.341, f32[2048]{0:T(1024)S(1)} %copy-done.28), channel_id=1, replica_groups=mesh['dp'=8,'tensor'=4] {'dp','tensor'}, use_global_device_ids=true, to_apply=%region_16.17 | all-reduce | flops 4096 | bytes 32768 | tf_op jit(solution)/shard_map/psum | solution.py:254
  1440.7 32.4 %reduce-scatter.14.cloned.1.call-done = bf16[256,2048]{1,0:T(8,128)(2,1)} async-done(((bf16[1024,2048]{1,0:T(8,128)(2,1)}), bf16[256,2048]{1,0:T(8,128)(2,1)}) %reduce-scatter.14.cloned.1.call-update) | async-done | bytes 1048592 | tf_op jit(solution)/shard_map/reduce_scatter | solution.py:163
  1473.1 5.1 fusion.76
  (210 shorter events, 75.4 us)
Async XLA Ops:
  7.2 5.7 copy-start.37
  7.2 5.7 copy-start.26
  7.2 17.1 %copy-start.27 = (bf16[256,128]{1,0:T(8,128)(2,1)S(1)}, bf16[256,128]{1,0:T(8,128)(2,1)}, u32[]{:S(2)}) copy-start(bf16[256,128]{1,0:T(8,128)(2,1)} %param.23) | copy-start | bytes 196612
  7.2 87.7 %all-gather.9.cloned.1.call-start = ((), (), s32[]{:S(2)}) async-start(), calls=%async_computation.11 | async-start | bytes 5242880 | tf_op jit(solution)/shard_map/all_gather | solution.py:90
  8.8 15.5 %copy-start.35 = (f32[256]{0:T(256)}, f32[256]{0:T(256)S(1)}, u32[]{:S(2)}) copy-start(f32[256]{0:T(256)S(1)} %fusion.77) | copy-start | bytes 3076
  8.8 15.5 %copy-start.31 = (f32[256]{0:T(256)}, f32[256]{0:T(256)S(1)}, u32[]{:S(2)}) copy-start(f32[256]{0:T(256)S(1)} %fusion.82) | copy-start | bytes 3076
  11.3 111.8 %all-gather.11.cloned.1.call-start = ((), (), s32[]{:S(2)}) async-start(), calls=%async_computation.12 | async-start | bytes 2359296 | tf_op jit(solution)/shard_map/all_gather | solution.py:92
  12.1 151.4 %all-gather.13.cloned.1.call-start = ((), (), s32[]{:S(2)}) async-start(), calls=%async_computation.13 | async-start | bytes 2359296 | tf_op jit(solution)/shard_map/all_gather | solution.py:95
  12.8 233.9 %reduce-scatter.12.cloned.1.call-start = ((), (), s32[]{:S(2)}) async-start(), calls=%async_computation.14 | async-start | bytes 5242880 | tf_op jit(solution)/shard_map/reduce_scatter | solution.py:146
  24.3 104.1 %copy-start.14 = (bf16[2048,128]{1,0:T(8,128)(2,1)}, bf16[2048,128]{1,0:T(8,128)(2,1)S(1)}, u32[]{:S(2)}) copy-start(bf16[2048,128]{1,0:T(8,128)(2,1)S(1)} %all_gather.32) | copy-start | bytes 1572868
  34.1 95.8 %copy-start.12 = (bf16[2048,128]{1,0:T(8,128)(2,1)}, bf16[2048,128]{1,0:T(8,128)(2,1)S(1)}, u32[]{:S(2)}) copy-start(bf16[2048,128]{1,0:T(8,128)(2,1)S(1)} %all_gather.33) | copy-start | bytes 1572868
  34.6 93.8 %copy-start.17 = (f32[1024,32]{0,1:T(8,128)}, f32[1024,32]{0,1:T(8,128)S(1)}, u32[]{:S(2)}) copy-start(f32[1024,32]{0,1:T(8,128)S(1)} %get-tuple-element.402) | copy-start | bytes 393220
  34.6 93.8 %copy-start.19 = (f32[1024,32]{0,1:T(8,128)}, f32[1024,32]{0,1:T(8,128)S(1)}, u32[]{:S(2)}) copy-start(f32[1024,32]{0,1:T(8,128)S(1)} %get-tuple-element.403) | copy-start | bytes 393220
  128.4 2.6 copy-start.5
  128.8 3.7 copy-start.21
  163.4 6.4 copy-start.7
  163.4 6.4 copy-start.40
  169.8 77.0 %copy-start.1 = (bf16[256,2048]{1,0:T(8,128)(2,1)S(1)}, bf16[256,2048]{1,0:T(8,128)(2,1)}, u32[]{:S(2)}) copy-start(bf16[256,2048]{1,0:T(8,128)(2,1)} %param.17) | copy-start | bytes 3145732
  169.8 78.6 %copy-start.23 = (f32[2048]{0:T(1024)S(1)}, f32[2048]{0:T(1024)}, u32[]{:S(2)}) copy-start(f32[2048]{0:T(1024)} %param.25) | copy-start | bytes 24580
  169.8 133.5 %all-gather.19.cloned.1.call-start = ((), (), s32[]{:S(2)}) async-start(), calls=%async_computation.17 | async-start | bytes 9437184 | tf_op jit(solution)/shard_map/all_gather | solution.py:157
  170.4 215.7 %all-gather.15.cloned.1.call-start = ((), (), s32[]{:S(2)}) async-start(), calls=%async_computation.15 | async-start | bytes 5242880 | tf_op jit(solution)/shard_map/all_gather | solution.py:154
  248.4 458.2 %copy-start.29 = (f32[256]{0:T(256)}, f32[256]{0:T(256)S(1)}, u32[]{:S(2)}) copy-start(f32[256]{0:T(256)S(1)} %fusion.83) | copy-start | bytes 3076
  251.0 189.7 %all-gather.17.cloned.1.call-start = ((), (), s32[]{:S(2)}) async-start(), calls=%async_computation.16 | async-start | bytes 9437184 | tf_op jit(solution)/shard_map/all_gather | solution.py:156
  251.8 271.3 %all-gather.23.cloned.1.call-start = ((), (), s32[]{:S(2)}) async-start(), calls=%async_computation.20 | async-start | bytes 5242880 | tf_op jit(solution)/shard_map/all_gather | solution.py:170
  252.5 326.8 %all-gather.21.cloned.1.call-start = ((), (), s32[]{:S(2)}) async-start(), calls=%async_computation.18 | async-start | bytes 9437184 | tf_op jit(solution)/shard_map/all_gather | solution.py:158
  253.3 450.6 %reduce-scatter.16.cloned.1.call-start = ((), (), s32[]{:S(2)}) async-start(), calls=%async_computation.21 | async-start | bytes 5242880 | tf_op jit(solution)/shard_map/reduce_scatter | solution.py:179
  601.1 12.9 copy-start.42
  626.9 77.0 %copy-start.3 = (bf16[256,2048]{1,0:T(8,128)(2,1)S(1)}, bf16[256,2048]{1,0:T(8,128)(2,1)}, u32[]{:S(2)}) copy-start(bf16[256,2048]{1,0:T(8,128)(2,1)} %reduce-scatter.12.cloned.1.call-done) | copy-start | bytes 3145732
  626.9 79.8 %copy-start.9 = (bf16[256,2048]{1,0:T(8,128)(2,1)S(1)}, bf16[256,2048]{1,0:T(8,128)(2,1)}, u32[]{:S(2)}) copy-start(bf16[256,2048]{1,0:T(8,128)(2,1)} %param.29) | copy-start | bytes 3145732
  626.9 386.8 %reduce-scatter.24.cloned.1.call-start = ((), (), s32[]{:S(2)}) async-start(), calls=%async_computation.25 | async-start | bytes 589824 | tf_op jit(solution)/shard_map/reduce_scatter | solution.py:262
  706.6 57.8 %copy-start.33 = (f32[256]{0:T(256)}, f32[256]{0:T(256)S(1)}, u32[]{:S(2)}) copy-start(f32[256]{0:T(256)S(1)} %multiply_multiply_fusion.1) | copy-start | bytes 3076
  709.8 26.6 %collective-permute-start = (bf16[256,2048]{1,0:T(8,128)(2,1)}, bf16[256,2048]{1,0:T(8,128)(2,1)S(1)}, u32[]{:S(2)}, u32[]{:S(2)}) collective-permute-start(bf16[256,2048]{1,0:T(8,128)(2,1)} %fusion.86), channel_id=1, source_target_pairs={{0,1},{1,2},{2,3},{3,0},{4,5},{5,6},{6,7},{7,4},{8,9},{9,10},{10,1... | collective-permute-start | bytes 3145736 | tf_op jit(solution)/shard_map/ppermute | solution.py:24
  736.4 27.8 %collective-permute-start.1 = (bf16[256,2048]{1,0:T(8,128)(2,1)S(1)}, bf16[256,2048]{1,0:T(8,128)(2,1)S(1)}, u32[]{:S(2)}, u32[]{:S(2)}) collective-permute-start(bf16[256,2048]{1,0:T(8,128)(2,1)S(1)} %collective-permute-done), channel_id=1, source_target_pairs={{0,1},{1,2},{2,3},{3,0},{4,5},{5,6},{6,7},{7,4},{8,9},{9,10},{10,1... | collective-permute-start | bytes 3145736 | tf_op jit(solution)/shard_map/ppermute | solution.py:24
  736.4 46.6 %collective-permute-start.2 = (bf16[256,2048]{1,0:T(8,128)(2,1)}, bf16[256,2048]{1,0:T(8,128)(2,1)S(1)}, u32[]{:S(2)}, u32[]{:S(2)}) collective-permute-start(bf16[256,2048]{1,0:T(8,128)(2,1)} %fusion.86), channel_id=1, source_target_pairs={{0,3},{1,0},{2,1},{3,2},{4,7},{5,4},{6,5},{7,6},{8,11},{9,8},{10,9... | collective-permute-start | bytes 3145736 | tf_op jit(solution)/shard_map/ppermute | solution.py:27
  785.0 3.7 copy-start.22
  785.0 3.7 copy-start.8
  793.2 4.0 copy-start.16
  793.7 3.5 copy-start.11
  821.6 3.2 copy-start
  859.0 4.0 copy-start.16
  859.5 3.5 copy-start.11
  888.4 3.2 copy-start
  922.1 5.5 copy-start.18
  922.2 5.5 copy-start.20
  927.6 87.7 %reduce-scatter.22.cloned.1.call-start = ((), (), s32[]{:S(2)}) async-start(), calls=%async_computation.24 | async-start | bytes 589824 | tf_op jit(solution)/shard_map/reduce_scatter | solution.py:259
  933.2 141.7 %reduce-scatter.30.cloned.1.call-start = ((), (), s32[]{:S(2)}) async-start(), calls=%async_computation.28 | async-start | bytes 9437184 | tf_op jit(solution)/shard_map/reduce_scatter | solution.py:271
  947.3 202.4 %reduce-scatter.28.cloned.1.call-start = ((), (), s32[]{:S(2)}) async-start(), calls=%async_computation.27 | async-start | bytes 9437184 | tf_op jit(solution)/shard_map/reduce_scatter | solution.py:268
  961.5 262.9 %reduce-scatter.32.cloned.1.call-start = ((), (), s32[]{:S(2)}) async-start(), calls=%async_computation.29 | async-start | bytes 9437184 | tf_op jit(solution)/shard_map/reduce_scatter | solution.py:274
  975.8 292.7 %reduce-scatter.26.cloned.1.call-start = ((), (), s32[]{:S(2)}) async-start(), calls=%async_computation.26 | async-start | bytes 2359296 | tf_op jit(solution)/shard_map/reduce_scatter | solution.py:265
  983.0 330.4 %reduce-scatter.20.cloned.1.call-start = ((), (), s32[]{:S(2)}) async-start(), calls=%async_computation.23 | async-start | bytes 2359296 | tf_op jit(solution)/shard_map/reduce_scatter | solution.py:256
  988.3 4.1 copy-start.15
  992.2 400.2 %reduce-scatter.18.cloned.1.call-start = ((), (), s32[]{:S(2)}) async-start(), calls=%async_computation.22 | async-start | bytes 5242880 | tf_op jit(solution)/shard_map/reduce_scatter | solution.py:241
  994.1 2.4 copy-start.13
  999.8 473.3 %reduce-scatter.14.cloned.1.call-start = ((), (), s32[]{:S(2)}) async-start(), calls=%async_computation.19 | async-start | bytes 5242880 | tf_op jit(solution)/shard_map/reduce_scatter | solution.py:163
  1077.6 314.8 %copy-start.2 = (bf16[256,2048]{1,0:T(8,128)(2,1)S(1)}, bf16[256,2048]{1,0:T(8,128)(2,1)}, u32[]{:S(2)}) copy-start(bf16[256,2048]{1,0:T(8,128)(2,1)} %param.17) | copy-start | bytes 3145732
  1077.6 314.8 %copy-start.25 = (f32[2048]{0:T(1024)S(1)}, f32[2048]{0:T(1024)}, u32[]{:S(2)}) copy-start(f32[2048]{0:T(1024)} %param.20) | copy-start | bytes 24580
  1077.6 314.8 %copy-start.32 = (f32[256]{0:T(256)S(1)}, f32[256]{0:T(256)}, u32[]{:S(2)}) copy-start(f32[256]{0:T(256)} %copy-done.31) | copy-start | bytes 3076
  1152.5 242.2 %copy-start.28 = (f32[2048]{0:T(1024)S(1)}, f32[2048]{0:T(1024)}, u32[]{:S(2)}) copy-start(f32[2048]{0:T(1024)} %get-tuple-element.339) | copy-start | bytes 24580
  1152.5 288.2 %copy-start.36 = (f32[256]{0:T(256)S(1)}, f32[256]{0:T(256)}, u32[]{:S(2)}) copy-start(f32[256]{0:T(256)} %copy-done.35) | copy-start | bytes 3076
  1152.5 320.6 %copy-start.4 = (bf16[256,2048]{1,0:T(8,128)(2,1)S(1)}, bf16[256,2048]{1,0:T(8,128)(2,1)}, u32[]{:S(2)}) copy-start(bf16[256,2048]{1,0:T(8,128)(2,1)} %reduce-scatter.12.cloned.1.call-done) | copy-start | bytes 3145732
  1152.5 320.7 %copy-start.10 = (bf16[256,2048]{1,0:T(8,128)(2,1)S(1)}, bf16[256,2048]{1,0:T(8,128)(2,1)}, u32[]{:S(2)}) copy-start(bf16[256,2048]{1,0:T(8,128)(2,1)} %param.29) | copy-start | bytes 3145732
  1152.5 320.6 %copy-start.24 = (f32[2048]{0:T(1024)S(1)}, f32[2048]{0:T(1024)}, u32[]{:S(2)}) copy-start(f32[2048]{0:T(1024)} %param.25) | copy-start | bytes 24580
  1152.5 320.6 %copy-start.30 = (f32[256]{0:T(256)S(1)}, f32[256]{0:T(256)}, u32[]{:S(2)}) copy-start(f32[256]{0:T(256)} %copy-done.29) | copy-start | bytes 3076
  1152.5 320.6 %copy-start.34 = (f32[256]{0:T(256)S(1)}, f32[256]{0:T(256)}, u32[]{:S(2)}) copy-start(f32[256]{0:T(256)} %copy-done.33) | copy-start | bytes 3076
  (4 other events, 6.9 us)
Sparse Core Ops, SparseCore 0:
  11.4 83.4 all-gather.8
  96.8 26.2 all-gather.10
  125.0 28.1 all-gather.12
  170.0 76.7 reduce-scatter.11
  248.5 54.7 all-gather.18
  305.3 80.7 all-gather.14
  388.0 52.7 all-gather.16
  442.3 80.7 all-gather.22
  525.0 54.3 all-gather.20
  627.0 76.7 reduce-scatter.15
  927.7 34.3 reduce-scatter.23
  965.7 34.1 reduce-scatter.21
  1003.3 71.4 reduce-scatter.29
  1078.1 71.4 reduce-scatter.27
  1153.0 71.2 reduce-scatter.31
  1227.4 41.0 reduce-scatter.25
  1272.3 41.1 reduce-scatter.19
  1315.6 76.7 reduce-scatter.17
  1394.7 78.3 reduce-scatter.13
